TPU v7x, 256 devices: a whole 4x4x8 slice. The times are simulated.
256 devices in a mesh: own: 16 (over x_hi, y, core), rep: 16 (over z, x_lo).
Axes of the slice: x: 4 (x_hi: 2, x_lo: 2; x = x_hi * 2 + x_lo), y: 4, z: 8, core: 2. Of those that a mesh axis runs over, the one named last changes fastest.
Arguments:
- latents: bfloat16 [512, 32, 32, 320], P(('own', 'rep')), may hold values from -6 to 6
- targets: bfloat16 [512, 32, 32, 320], P(('own', 'rep')), may hold values from -6 to 6
- advantages: float32 [512], P(('own', 'rep')), may hold values from -4 to 4
- timesteps: int32 [512], P(('own', 'rep')), may hold values from 0 to 49
- kernel: bfloat16 [2880, 320], replicated, may hold values from -0.109375 to 0.109375
- prior_left: float32 [16, 180, 180], P('own'), as said below
- prior_right: float32 [16, 320, 320], P('own'), as said below
Outputs:
- step: bfloat16 [2880, 320], replicated
Inputs may be any that keep to these rules, and one draw needn't show every extreme that they name: `prior_left`: each block is symmetric positive definite. `prior_right`: each block is symmetric positive definite.
All inputs are finite; a program needn't handle non-finite values.
Results may differ from a plain program's by a relative error of at most 0.0049.
Values may be sent and summed in bfloat16 or wider, within the bound.
No kernel may reach another device: no remote copies, remote signals or barrier semaphores. Data moves between devices by JAX's collectives and lax.ppermute only.
A program may use at most 128 MiB of HBM per device.

v0:
```python
import jax
import jax.numpy as jnp
from jax import lax
from jax.sharding import PartitionSpec as P

ITERS = 8
STEPS = 50


momentum_beta = 0.9


def unfold_taps(images):
    height = images.shape[1]
    breadth = images.shape[2]
    padded = jnp.pad(images, ((0, 0), (1, 1), (1, 1), (0, 0)))
    pieces = [
        padded[:, row_off : row_off + height, col_off : col_off + breadth, :]
        for row_off in range(3)
        for col_off in range(3)
    ]
    stacked = jnp.concatenate(pieces, axis=-1)
    return stacked.reshape(-1, 9 * images.shape[3])


def inverse_root(matrix):
    order = matrix.shape[-1]
    identity = jnp.eye(order, dtype=jnp.float32)[None]
    frob_scale = jnp.sqrt(jnp.sum(matrix * matrix, axis=(1, 2), keepdims=True))
    iterate = matrix / frob_scale
    root_now = identity
    for sweep in range(ITERS):
        middle = 1.5 * identity - 0.5 * jnp.einsum(
            "bij,bjk->bik", root_now, iterate, precision=lax.Precision.HIGHEST
        )
        iterate = jnp.einsum("bij,bjk->bik", iterate, middle, precision=lax.Precision.HIGHEST)
        root_now = jnp.einsum("bij,bjk->bik", middle, root_now, precision=lax.Precision.HIGHEST)
    return root_now


def local(latents, targets, advantages, timesteps, kernel, prior_left, prior_right):
    samples_here = latents.shape[0]
    spots = latents.shape[1] * latents.shape[2]
    chans = latents.shape[3]
    kernel_rows = kernel.shape[0]
    owners = lax.axis_size("own")
    replicas = lax.axis_size("rep")
    total = float(samples_here * spots * owners * replicas)
    columns = unfold_taps(latents)
    output = jnp.dot(columns, kernel, preferred_element_type=jnp.float32)
    scaled = advantages / ((0.1 + timesteps.astype(jnp.float32) / STEPS) * total)
    diffs = output.reshape(samples_here, spots, chans) - targets.reshape(
        samples_here, spots, chans
    ).astype(jnp.float32)
    cotangent = (scaled[:, None, None] * diffs).astype(jnp.bfloat16).reshape(-1, chans)
    rows_owned = kernel_rows // owners
    owned = lax.psum_scatter(
        lax.dot_general(
            columns, cotangent, (((0,), (0,)), ((), ())), preferred_element_type=jnp.float32
        ),
        "own",
        scatter_dimension=0,
        tiled=True,
    )
    owned = lax.psum(owned, "rep")
    block_rows = prior_left.shape[1]
    blocks = owned.reshape(-1, block_rows, chans)
    new_left = momentum_beta * prior_left + jnp.einsum(
        "bij,bkj->bik", blocks, blocks, precision=lax.Precision.HIGHEST
    )
    new_right = momentum_beta * prior_right + jnp.einsum(
        "bji,bjk->bik", blocks, blocks, precision=lax.Precision.HIGHEST
    )
    root_left = inverse_root(new_left)
    root_right = inverse_root(new_right)
    update = jnp.einsum("bij,bjk->bik", root_left, blocks, precision=lax.Precision.HIGHEST)
    update = jnp.einsum("bij,bjk->bik", update, root_right, precision=lax.Precision.HIGHEST)
    spread_sq = jnp.mean(update * update, axis=(1, 2), keepdims=True)
    step_owned = (
        (update / jnp.sqrt(spread_sq + 1e-06)).astype(jnp.bfloat16).reshape(rows_owned, chans)
    )
    step_full = lax.all_gather(step_owned, "own", axis=0, tiled=True)
    return step_full


def solution(mesh):
    placed = (
        P(("own", "rep"), None, None, None),
        P(("own", "rep"), None, None, None),
        P(("own", "rep")),
        P(("own", "rep")),
        P(),
        P("own", None, None),
        P("own", None, None),
    )
    return jax.shard_map(local, mesh=mesh, in_specs=placed, out_specs=P(), check_vma=False)
```

profile of v0, /device:TPU:1, one launch (start us, length us, event | category | flops | bytes accessed | tf_op | source)
XLA Modules:
  0.0 374.2 jit_solution(9797892050429937504)
XLA Ops:
  6.5 12.2 %pad_slice_fusion = (bf16[2,32,32,320]{3,2,1,0:T(8,128)(2,1)}, bf16[2,32,32,320]{3,2,1,0:T(8,128)(2,1)}, bf16[2,32,32,320]{3,2,1,0:T(8,128)(2,1)}, bf16[2,32,32,...) fusion(bf16[2,32,32,320]{3,2,1,0:T(8,128)(2,1)} %param.7), kind=kLoop, calls=%fused_computation.1 | loop fusion | bytes 11796480 | tf_op jit(solution)/shard_map/slice | solution.py:18
  18.8 2.0 bitcast_convert_fusion
  20.8 3.5 copy.19
  24.3 19.3 %concatenate.3 = bf16[2,32,32,2880]{3,2,1,0:T(8,128)(2,1)} concatenate(bf16[2,32,32,320]{3,2,1,0:T(8,128)(2,1)} %get-tuple-element.12, bf16[2,32,32,320]{3,2,1,0:T(8,128)(2,1)} %get-tuple-element.6, bf16[2,32,32,320]{3,2,1,0:T(8,128)(2,1)} %get-tuple-element.7, bf16[2,32,32,320]{3,2,1,0:T(8,128)(2,1)} %get-tuple-element.8, bf16[2,32,32,320]{3,2,1,0:T(8,128)(2,1)S(1)} %copy-done.4, ...), dimensions={3} | concatenate | bytes 23592960 | tf_op jit(solution)/shard_map/concatenate | solution.py:22
  43.6 13.4 %fusion.5 = bf16[2,40,8,1024]{3,2,1,0:T(8,128)(2,1)S(1)} fusion(f32[2,1024,320]{1,2,0:T(8,128)} %copy.19, bf16[2,1024,2880]{2,1,0:T(8,128)(2,1)} %bitcast.133, bf16[2880,320]{0,1:T(8,128)(2,1)S(1)} %copy-done, f32[2]{0:T(128)S(1)} %multiply_divide_fusion), kind=kOutput, calls=%fused_computation.20 | convolution fusion | flops 3776839680 | bytes 17571848 | tf_op jit(solution)/shard_map/dot_general | solution.py:50
  57.2 8.7 %fusion.27 = f32[2880,320]{1,0:T(8,128)} fusion(bf16[2048,2880]{1,0:T(8,128)(2,1)S(1)} %bitcast.134, bf16[2048,320]{0,1:T(8,128)(2,1)S(1)} %bitcast.135), kind=kOutput, calls=%fused_computation.69 | convolution fusion | flops 3774873600 | bytes 16793600 | tf_op jit(solution)/shard_map/dot_general | solution.py:58
  65.9 48.6 %fusion = f32[192,320]{1,0:T(8,128)S(1)} fusion(f32[2880,320]{1,0:T(8,128)} %fusion.27), kind=kCustom, calls=%all-reduce-scatter | all-reduce-scatter fusion | flops 983041 | bytes 3933184
  114.5 2.6 collective-permute-start
  118.4 4.6 %collective-permute-done = f32[180,320]{1,0:T(8,128)S(1)} collective-permute-done((f32[180,320]{1,0:T(8,128)S(1)}, f32[180,320]{1,0:T(8,128)S(1)}, u32[]{:S(2)}, u32[]{:S(2)}) %collective-permute-start) | collective-permute-done | bytes 230432
  124.8 131.9 %all-reduce.5.cloned.1.call-done = f32[180,320]{1,0:T(8,128)} async-done(((f32[180,320]{1,0:T(8,128)}), f32[180,320]{1,0:T(8,128)}) %all-reduce.5.cloned.1.call-update) | async-done | bytes 230416 | tf_op jit(solution)/shard_map/psum | solution.py:65
  256.7 2.6 multiply_reduce_fusion
  260.6 1.1 fusion.18
  262.3 1.1 select_subtract_fusion.6
  263.4 1.1 fusion.43
  264.4 1.1 fusion.42
  265.5 1.1 select_subtract_fusion.5
  266.6 1.1 fusion.45
  268.8 1.1 select_subtract_fusion.4
  269.9 1.1 fusion.47
  271.0 1.3 fusion.46
  272.3 1.1 select_subtract_fusion.3
  276.6 1.1 fusion.51
  277.7 1.1 fusion.50
  278.8 1.1 select_subtract_fusion.1
  281.0 1.1 fusion.52
  282.1 1.1 multiply_reduce_fusion.2
  290.7 1.1 select_subtract_fusion
  291.8 1.1 fusion.54
  294.0 1.4 multiply_reduce_fusion.1
  296.8 62.0 %all-gather.3.cloned.1.call-done = bf16[16,180,320]{2,1,0:T(8,128)(2,1)} async-done(((bf16[1,180,320]{2,1,0:T(8,128)(2,1)}), bf16[16,180,320]{2,1,0:T(8,128)(2,1)}) %all-gather.3.cloned.1.call-update) | async-done | bytes 1843216 | tf_op jit(solution)/shard_map/all_gather | solution.py:82
  358.8 4.3 %reshape.339 = bf16[2880,320]{1,0:T(8,128)(2,1)} reshape(bf16[16,180,320]{2,1,0:T(8,128)(2,1)} %all-gather.3.cloned.1.call-done) | data formatting | bytes 3686400
  363.1 4.0 %copy.21 = bf16[2880,320]{0,1:T(8,128)(2,1)} copy(bf16[2880,320]{1,0:T(8,128)(2,1)} %reshape.339) | data formatting | bytes 3686400
  (64 shorter events, 17.6 us)
Async XLA Ops:
  6.5 37.1 %copy-start = (bf16[2880,320]{0,1:T(8,128)(2,1)S(1)}, bf16[2880,320]{0,1:T(8,128)(2,1)}, u32[]{:S(2)}) copy-start(bf16[2880,320]{0,1:T(8,128)(2,1)} %param.11) | copy-start | bytes 5529604
  6.5 12.2 %copy-start.5 = (bf16[2,32,32,320]{3,2,1,0:T(8,128)(2,1)S(1)}, bf16[2,32,32,320]{3,2,1,0:T(8,128)(2,1)}, u32[]{:S(2)}) copy-start(bf16[2,32,32,320]{3,2,1,0:T(8,128)(2,1)} %param.8) | copy-start | bytes 3932164
  6.5 250.2 %all-reduce.5.cloned.1.call-start = ((), (), s32[]{:S(2)}) async-start(), calls=%async_computation | async-start | bytes 565248 | tf_op jit(solution)/shard_map/psum | solution.py:65
  20.8 3.5 copy-start.9
  20.8 3.5 copy-start.10
  20.8 3.5 copy-start.4
  43.6 13.6 %copy-start.2 = (bf16[2,32,32,2880]{3,2,1,0:T(8,128)(2,1)S(1)}, bf16[2,32,32,2880]{3,2,1,0:T(8,128)(2,1)}, u32[]{:S(2)}) copy-start(bf16[2,32,32,2880]{3,2,1,0:T(8,128)(2,1)} %concatenate.3) | copy-start | bytes 35389444
  65.9 51.3 %copy-start.8 = (u32[256]{0:T(256)S(1)}, u32[256]{0:T(256)}, u32[]{:S(2)}) copy-start(u32[256]{0:T(256)} %constant.40) | copy-start | bytes 3076
  114.5 142.3 %copy-start.6 = (f32[1,320,320]{2,1,0:T(8,128)S(1)}, f32[1,320,320]{2,1,0:T(8,128)}, u32[]{:S(2)}) copy-start(f32[1,320,320]{2,1,0:T(8,128)} %param.13) | copy-start | bytes 1228804
  114.5 8.5 %collective-permute-start = (f32[180,320]{1,0:T(8,128)S(1)}, f32[180,320]{1,0:T(8,128)S(1)}, u32[]{:S(2)}, u32[]{:S(2)}) collective-permute-start(f32[180,320]{1,0:T(8,128)S(1)} %slice.33), channel_id=1, source_target_pairs={{0,16},{16,32},{32,48},{48,64},{64,80},{80,96},{96,112},{112,128},... | collective-permute-start | bytes 691208
  124.3 234.5 %all-gather.3.cloned.1.call-start = ((), (), s32[]{:S(2)}) async-start(), calls=%async_computation.1 | async-start | bytes 2402304 | tf_op jit(solution)/shard_map/all_gather | solution.py:82
  278.8 3.3 copy-start.3
  278.8 3.3 copy-start.7
  358.8 8.3 %copy-start.1 = (bf16[2880,320]{0,1:T(8,128)(2,1)S(1)}, bf16[2880,320]{0,1:T(8,128)(2,1)}, u32[]{:S(2)}) copy-start(bf16[2880,320]{0,1:T(8,128)(2,1)} %param.11) | copy-start | bytes 5529604
Sparse Core Ops, SparseCore 0:
  124.5 132.2 all-reduce.4
  296.9 61.8 all-gather.2
where the time goes:
time: 381 us; the launch traced here: 374 us
  waiting for transfers between devices  199 us (52%)
  matrix products  59 us (15%)
  blocking collectives  48.6 us (13%)
  local copies, waits for them, and re-layouts  45.4 us (12%)
  between operations  16.9 us (4%)
    psum x1, waiting for transfers between devices, local(): owned = lax.psum(owned, 'rep')  132 us
    all_gather x1, waiting for transfers between devices, local(): step_full = lax.all_gather(step_owned, 'own', axis=0, tiled=True)  62 us
    unnamed x1, blocking collectives  48.6 us
    concatenate x1, local copies, waits for them, and re-layouts, unfold_taps(): stacked = jnp.concatenate(pieces, axis=-1)  19.3 us
    dot_general x1, matrix products, local(): output = jnp.dot(columns, kernel, preferred_element_type=jnp.float32)  13.4 us
    slice x1, local copies, waits for them, and re-layouts, unfold_taps(): padded[:, row_off:row_off + height, col_off:col_off + breadth, :]  12.2 us
    dot_general x16, matrix products, inverse_root(): jnp.einsum('bij,bjk->bik', root_now, iterate, precision=lax.Precision.HIG...  10.9 us
    dot_general x16, matrix products, inverse_root(): jnp.einsum('bij,bjk->bik', middle, root_now, precision=lax.Precision.HIGH...  10.7 us
  transfers between devices with their start and end apart: 3, of which 3 were waited for; matrix products, arithmetic and copies ran while one was open for 0% of the time, Pallas kernels for 0%

commit v1 on v0

v1 whole, which is shorter than its diff:
```python
import functools

import jax
import jax.numpy as jnp
from jax import lax
from jax.experimental import pallas as pl
from jax.experimental.pallas import tpu as pltpu
from jax.sharding import PartitionSpec as P

ITERS = 8
STEPS = 50
BETA = 0.9
C = 320
SIDE = 32
SPOTS = 1024
ROWS = 2880
BROWS = 180
BLOCKS = 16
TRIPLE = 3 * C
STRIDE = SPOTS + 2 * SIDE
QROWS = 80
QPACK = 120
bf16 = jnp.bfloat16
f32 = jnp.float32

VMEM = pl.BlockSpec(memory_space=pltpu.VMEM)
SMEM = pl.BlockSpec(memory_space=pltpu.SMEM)


def dot(a, b, contract=(1, 0)):
    return lax.dot_general(
        a, b, (((contract[0],), (contract[1],)), ((), ())), preferred_element_type=f32
    )


def pack_block(block):
    pieces = []
    for q in range(4):
        rows = block[q * QROWS : (q + 1) * QROWS]
        half = QROWS // 2
        tail = jnp.concatenate(
            [
                rows[:half, 128:],
                jnp.zeros((half, 12), block.dtype),
                rows[half:, 128:],
                jnp.zeros((half, 12), block.dtype),
            ],
            axis=1,
        )
        pieces.append((rows[:, :128], tail))
    return pieces


def unpack_quarter(packed):
    half = QROWS // 2
    tail = packed[QROWS:]
    right = jnp.concatenate([tail[:, :52], tail[:, 64:116]], axis=0)
    return jnp.concatenate([packed[:QROWS], right], axis=1)


def conv_kernel(total, core_ref, adv_ref, time_ref, lat_ref, tgt_ref, ker_ref, out_ref, wide, kthree, cot, gt, minus):
    zeros = jnp.zeros((SIDE, TRIPLE), bf16)
    for s in range(2):
        wide[s * STRIDE : s * STRIDE + SIDE, :] = zeros
        wide[s * STRIDE + SIDE + SPOTS : (s + 1) * STRIDE, :] = zeros
    chunk = 128
    column = lax.broadcasted_iota(jnp.int32, (chunk, C), 0) % SIDE

    for s in range(2):

        def widen(i, carry, s=s):
            x = lat_ref[pl.ds(pl.multiple_of(s * SPOTS + i * chunk, chunk), chunk), :].astype(f32)
            before = jnp.where(column == 0, 0.0, pltpu.roll(x, 1, 0))
            after = jnp.where(column == SIDE - 1, 0.0, pltpu.roll(x, chunk - 1, 0))
            row = pl.multiple_of(s * STRIDE + SIDE + i * chunk, 32)
            wide[pl.ds(row, chunk), :] = jnp.concatenate([before, x, after], axis=1).astype(bf16)
            return carry

        lax.fori_loop(0, SPOTS // chunk, widen, 0)
    for a in range(3):
        kthree[a] = ker_ref[:, a * TRIPLE : (a + 1) * TRIPLE]
    rows = lax.broadcasted_iota(jnp.int32, (C, C), 0)
    cols = lax.broadcasted_iota(jnp.int32, (C, C), 1)
    minus[...] = jnp.where(rows == cols, -1.0, 0.0).astype(bf16)

    span = 256
    for s in range(2):
        weight = jnp.full((1, span), adv_ref[s], f32) / (
            (0.1 + jnp.full((1, span), time_ref[s], jnp.int32).astype(f32) / STEPS) * total
        )

        def forward(j, carry, s=s, weight=weight):
            acc = dot(
                minus[...],
                tgt_ref[pl.ds(pl.multiple_of(s * SPOTS + j * span, span), span), :],
                (1, 1),
            )
            for a in range(3):
                row = pl.multiple_of(s * STRIDE + j * span + a * SIDE, 32)
                acc = acc + dot(kthree[a], wide[pl.ds(row, span), :], (1, 1))
            cot[:, pl.ds(pl.multiple_of(s * SPOTS + j * span, span), span)] = (weight * acc).astype(bf16)
            return carry

        lax.fori_loop(0, SPOTS // span, forward, 0)

    for a in range(3):
        for start in range(0, TRIPLE, 256):
            stop = min(start + 256, TRIPLE)
            acc = dot(cot[:, :SPOTS], wide[a * SIDE : a * SIDE + SPOTS, start:stop])
            acc = acc + dot(cot[:, SPOTS:], wide[STRIDE + a * SIDE : STRIDE + a * SIDE + SPOTS, start:stop])
            gt[a, :, start:stop] = acc

    core = core_ref[0]
    for b in range(BLOCKS):
        first, last = b * BROWS, (b + 1) * BROWS
        a = first // TRIPLE
        if last <= (a + 1) * TRIPLE:
            block = gt[a, :, first - a * TRIPLE : last - a * TRIPLE]
        else:
            edge = (a + 1) * TRIPLE
            block = jnp.concatenate(
                [gt[a, :, first - a * TRIPLE : TRIPLE], gt[a + 1, :, 0 : last - edge]], axis=1
            )
        slot = lax.bitwise_xor(core, jnp.int32(b % 2))
        for q, (head, tail) in enumerate(pack_block(block)):
            base = (b // 2) * 4 + q
            out_ref[slot, base, 0:QROWS, :] = head
            out_ref[slot, base, QROWS:QPACK, :] = tail


def conv_grad(total, core, advantages, timesteps, latents, targets, kernel_t):
    return pl.pallas_call(
        functools.partial(conv_kernel, total),
        out_shape=jax.ShapeDtypeStruct((2, 32, QPACK, 128), f32),
        in_specs=[SMEM, SMEM, SMEM, VMEM, VMEM, VMEM],
        out_specs=VMEM,
        scratch_shapes=[
            pltpu.VMEM((2 * STRIDE, TRIPLE), bf16),
            pltpu.VMEM((3, C, TRIPLE), bf16),
            pltpu.VMEM((C, 2 * SPOTS), bf16),
            pltpu.VMEM((3, C, TRIPLE), f32),
            pltpu.VMEM((C, C), bf16),
        ],
        compiler_params=pltpu.CompilerParams(vmem_limit_bytes=40 * 1024 * 1024),
        name="conv_grad",
    )(core, advantages, timesteps, latents, targets, kernel_t)


def halves(x):
    high = x.astype(bf16)
    return high, (x - high.astype(f32)).astype(bf16)


def left_operand(x):
    high, low = halves(x)
    return jnp.concatenate([high, high, low], axis=1)


def right_operand(x):
    high, low = halves(x)
    return jnp.concatenate([high, low, high], axis=0)


def eye(n):
    return jnp.where(
        lax.broadcasted_iota(jnp.int32, (n, n), 0) == lax.broadcasted_iota(jnp.int32, (n, n), 1),
        1.0,
        0.0,
    ).astype(f32)


def unit(matrix):
    total = jnp.sum(jnp.sum(matrix * matrix, axis=1, keepdims=True), axis=0, keepdims=True)
    return matrix / jnp.sqrt(total)


def shampoo_kernel(got_ref, left_ref, right_ref, out_ref, pr, plft, xs):
    quarters = []
    for q in range(4):
        s = got_ref[q].astype(f32)
        for z in range(1, 4):
            s = s + got_ref[4 * z + q].astype(f32)
        quarters.append(unpack_quarter(s))
    h = jnp.concatenate(quarters, axis=0)
    ht = h.T
    xs[...] = h
    pr[...] = unit(BETA * right_ref[...] + dot(left_operand(h), right_operand(ht)))
    plft[...] = unit(BETA * left_ref[...] + dot(left_operand(ht), right_operand(h)))

    def poly(p, square):
        n = p.shape[0]
        return 2.25 * eye(n) - 1.5 * p + 0.25 * square

    def sweep(i, carry):
        p = pr[...]
        x = xs[...]
        p3 = left_operand(p)
        both = dot(p3, right_operand(jnp.concatenate([p, x], axis=1)))
        x = 1.5 * x - 0.5 * both[:, C:]
        pr[...] = dot(p3, right_operand(poly(p, both[:, :C])))
        m = plft[...]
        m3 = right_operand(m)
        both = dot(left_operand(jnp.concatenate([x, m], axis=0)), m3)
        xs[...] = 1.5 * x - 0.5 * both[:C]
        plft[...] = dot(left_operand(m), right_operand(poly(m, both[C:])))
        return carry

    lax.fori_loop(0, ITERS - 1, sweep, 0)
    x = xs[...]
    x = 1.5 * x - 0.5 * dot(left_operand(pr[...]), right_operand(x))
    x = 1.5 * x - 0.5 * dot(left_operand(x), right_operand(plft[...]))
    mean = jnp.sum(jnp.sum(x * x, axis=1, keepdims=True), axis=0, keepdims=True) / (C * BROWS)
    x = x / jnp.sqrt(mean + 1e-06)
    for q, (head, tail) in enumerate(pack_block(x)):
        out_ref[q * QPACK : q * QPACK + QROWS, :] = head.astype(bf16)
        out_ref[q * QPACK + QROWS : (q + 1) * QPACK, :] = tail.astype(bf16)


def shampoo(got, left, right):
    return pl.pallas_call(
        shampoo_kernel,
        out_shape=jax.ShapeDtypeStruct((4 * QPACK, 128), bf16),
        in_specs=[VMEM, VMEM, VMEM],
        out_specs=VMEM,
        scratch_shapes=[
            pltpu.VMEM((C, C), f32),
            pltpu.VMEM((BROWS, BROWS), f32),
            pltpu.VMEM((C, BROWS), f32),
        ],
        compiler_params=pltpu.CompilerParams(vmem_limit_bytes=40 * 1024 * 1024),
        name="shampoo",
    )(got, left, right)


def join_kernel(core_ref, mine_ref, theirs_ref, out_ref):
    core = core_ref[0]

    def write(even, odd):
        for q in range(4):
            pieces = []
            for b in range(BLOCKS):
                source = even if b % 2 == 0 else odd
                packed = source[b // 2, q * QPACK : (q + 1) * QPACK, :].astype(f32)
                pieces.append(unpack_quarter(packed))
            out_ref[q * QROWS : (q + 1) * QROWS, :] = jnp.concatenate(pieces, axis=1).astype(bf16)

    @pl.when(core == 0)
    def _():
        write(mine_ref, theirs_ref)

    @pl.when(core == 1)
    def _():
        write(theirs_ref, mine_ref)


def join(core, mine, theirs):
    return pl.pallas_call(
        join_kernel,
        out_shape=jax.ShapeDtypeStruct((C, ROWS), bf16),
        in_specs=[SMEM, VMEM, VMEM],
        out_specs=VMEM,
        compiler_params=pltpu.CompilerParams(vmem_limit_bytes=40 * 1024 * 1024),
        name="join",
    )(core, mine, theirs)


CORE_SWAP = [(b, b ^ 1) for b in range(16)]
EIGHTS = [[2 * k + c for k in range(8)] for c in range(2)]
WIDE_GROUPS = [
    [(2 * k + c) * 16 + 4 * z + q for k in range(8) for q in range(4)]
    for c in range(2)
    for z in range(4)
]


def local(latents, targets, advantages, timesteps, kernel, prior_left, prior_right):
    core = (lax.axis_index("own") % 2).astype(jnp.int32).reshape(1)
    total = float(2 * SPOTS * lax.axis_size("own") * lax.axis_size("rep"))
    parts = conv_grad(
        total,
        core,
        advantages,
        timesteps,
        latents.reshape(2 * SPOTS, C),
        targets.reshape(2 * SPOTS, C),
        kernel.T,
    )
    theirs = lax.ppermute(parts[1].astype(bf16), "own", CORE_SWAP)
    pair = (parts[0] + theirs.astype(f32)).astype(bf16)
    spread = lax.all_to_all(pair, ("own", "rep"), 0, 0, axis_index_groups=WIDE_GROUPS)
    quarter = jnp.sum(spread.astype(f32), axis=0).astype(bf16)
    got = lax.all_to_all(jnp.broadcast_to(quarter, (16, QPACK, 128)), "rep", 0, 0)
    step = shampoo(got, prior_left[0], prior_right[0])
    mine = lax.all_to_all(
        jnp.broadcast_to(step, (8, 4 * QPACK, 128)), "own", 0, 0, axis_index_groups=EIGHTS
    )
    theirs = lax.ppermute(mine, "own", CORE_SWAP)
    return join(core, mine, theirs).T


def solution(mesh):
    placed = (
        P(("own", "rep"), None, None, None),
        P(("own", "rep"), None, None, None),
        P(("own", "rep")),
        P(("own", "rep")),
        P(),
        P("own", None, None),
        P("own", None, None),
    )
    return jax.shard_map(local, mesh=mesh, in_specs=placed, out_specs=P(), check_vma=False)
```

time: 381 us -> 109 us (0.29); the launches traced: 374 us -> 109 us
  waiting for transfers between devices: 199 us -> 18.6 us
  matrix products: 59 us -> 0 us
  local copies, waits for them, and re-layouts: 45.4 us -> 6.77 us
  Pallas kernels: 0 us -> 28.1 us
  between operations: 16.9 us -> 0.08 us
  starting transfers between devices: 3.1 us -> 16.2 us
  blocking collectives: 48.6 us -> 38.7 us
    psum x1 -> x0, waiting for transfers between devices: 132 us -> none  [local(): owned = lax.psum(owned, 'rep')]
    all_gather x1 -> x0, waiting for transfers between devices: 62 us -> none  [local(): step_full = lax.all_gather(step_owned, 'own', axis=0, tiled=True)]
    dot_general x52 -> x0, matrix products: 59 us -> none  [the longest x1 13.4 us: local(): output = jnp.dot(columns, kernel, preferred_element_type=jnp.float32)]
    unnamed x1 -> x0, blocking collectives: 48.6 us -> none
    all_to_all x0 -> x2, blocking collectives: none -> 38.7 us  [the longest x1 21.7 us: local(): lax.all_to_all(pair, ('own', 'rep'), 0, 0, axis_index_groups=WIDE_GROUPS)]
    pallas_call x0 -> x3, Pallas kernels: none -> 28.1 us  [the longest x1 13.4 us: conv_grad(): pl.pallas_call(functools.partial(conv_kernel, total), out_shape=jax.Shape...]
    concatenate x1 -> x0, local copies, waits for them, and re-layouts: 19.3 us -> none  [unfold_taps(): stacked = jnp.concatenate(pieces, axis=-1)]
    all_to_all x0 -> x1, waiting for transfers between devices: none -> 14.2 us  [local(): lax.all_to_all(jnp.broadcast_to(quarter, (16, QPACK, 128)), 'rep', 0, 0)]
where the time goes in v1:
time: 109 us
  blocking collectives  38.7 us (36%)
  Pallas kernels  28.1 us (26%)
  waiting for transfers between devices  18.6 us (17%)
  starting transfers between devices  16.2 us (15%)
  local copies, waits for them, and re-layouts  6.77 us (6%)
    all_to_all x1, blocking collectives, local(): lax.all_to_all(pair, ('own', 'rep'), 0, 0, axis_index_groups=WIDE_GROUPS)  21.7 us
    all_to_all x1, blocking collectives, local(): lax.all_to_all(jnp.broadcast_to(step, (8, 4 * QPACK, 128)), 'own', 0, 0,...  17 us
    all_to_all x1, waiting for transfers between devices, local(): lax.all_to_all(jnp.broadcast_to(quarter, (16, QPACK, 128)), 'rep', 0, 0)  14.2 us
    pallas_call x1, Pallas kernels, conv_grad(): pl.pallas_call(functools.partial(conv_kernel, total), out_shape=jax.Shape...  13.4 us
    pallas_call x1, Pallas kernels, shampoo(): pl.pallas_call(shampoo_kernel, out_shape=jax.ShapeDtypeStruct((4 * QPACK,...  12.4 us
    all_to_all x1, starting transfers between devices, local(): lax.all_to_all(jnp.broadcast_to(quarter, (16, QPACK, 128)), 'rep', 0, 0)  8.2 us
    unnamed x15, local copies, waits for them, and re-layouts  5.67 us
    ppermute x1, starting transfers between devices, local(): theirs = lax.ppermute(mine, 'own', CORE_SWAP)  4.7 us
  transfers between devices with their start and end apart: 3, of which 3 were waited for; matrix products, arithmetic and copies ran while one was open for 0% of the time, Pallas kernels for 0%

profile of v1, /device:TPU:1, one launch (start us, length us, event | category | flops | bytes accessed | tf_op | source)
XLA Modules:
  0.0 108.8 jit_solution(2675243907506094936)
XLA Ops:
  0.0 0.0 copy-start
  0.0 1.5 %copy-done = bf16[2880,320]{0,1:T(8,128)(2,1)S(1)} copy-done((bf16[2880,320]{0,1:T(8,128)(2,1)S(1)}, bf16[2880,320]{0,1:T(8,128)(2,1)}, u32[]{:S(2)}) %copy-start) | copy-done | bytes 1843224
  1.5 0.0 copy-start.1
  1.5 1.4 %copy-done.1 = bf16[2,32,32,320]{3,2,1,0:T(8,128)(2,1)S(1)} copy-done((bf16[2,32,32,320]{3,2,1,0:T(8,128)(2,1)S(1)}, bf16[2,32,32,320]{3,2,1,0:T(8,128)(2,1)}, u32[]{:S(2)}) %copy-start.1) | copy-done | bytes 1310744
  2.9 0.0 copy-start.2
  2.9 1.4 %copy-done.2 = bf16[2,32,32,320]{3,2,1,0:T(8,128)(2,1)S(1)} copy-done((bf16[2,32,32,320]{3,2,1,0:T(8,128)(2,1)S(1)}, bf16[2,32,32,320]{3,2,1,0:T(8,128)(2,1)}, u32[]{:S(2)}) %copy-start.2) | copy-done | bytes 1310744
  4.3 0.0 copy-start.4
  4.3 0.7 copy-done.4
  5.0 0.0 copy-start.5
  5.0 0.7 copy-done.5
  5.6 13.4 %conv_grad.1 = f32[2,32,120,128]{3,2,1,0:T(8,128)S(1)} custom-call(s32[1]{0:T(128)} %bitcast.core_ref, f32[2]{0:T(128)S(1)} %copy-done.4, s32[2]{0:T(128)S(1)} %copy-done.5, bf16[2048,320]{1,0:T(8,128)(2,1)S(1)} %bitcast.18, bf16[2048,320]{1,0:T(8,128)(2,1)S(1)} %bitcast.19, bf16[320,2880]{1,0:T(8,128)(2,1)S(1)} %bitcast.17), custom_call_target="tpu_custom_call" | custom-call | tf_op jit(solution)/shard_map/conv_grad/pallas_call | solution.py:132
  19.1 0.1 fusion.2
  19.2 3.3 %collective-permute-start = (bf16[32,120,128]{2,1,0:T(8,128)(2,1)S(1)}, bf16[32,120,128]{2,1,0:T(8,128)(2,1)S(1)}, u32[]{:S(2)}, u32[]{:S(2)}) collective-permute-start(bf16[32,120,128]{2,1,0:T(8,128)(2,1)S(1)} %fusion.2), channel_id=1, source_target_pairs={{0,16},{16,0},{32,48},{48,32},{64,80},{80,64},{96,112},{112,96},{1... | collective-permute-start | bytes 2949128 | tf_op jit(solution)/shard_map/ppermute | solution.py:288
  22.5 2.2 %collective-permute-done = bf16[32,120,128]{2,1,0:T(8,128)(2,1)S(1)} collective-permute-done((bf16[32,120,128]{2,1,0:T(8,128)(2,1)S(1)}, bf16[32,120,128]{2,1,0:T(8,128)(2,1)S(1)}, u32[]{:S(2)}, u32[]{:S(2)}) %collective-permute-start) | collective-permute-done | bytes 983072 | tf_op jit(solution)/shard_map/ppermute | solution.py:288
  24.7 0.2 fusion.1
  24.9 0.0 copy-start.6
  24.9 0.0 copy-start.3
  24.9 21.7 %all_to_all.15 = bf16[32,120,128]{2,1,0:T(8,128)(2,1)S(1)} all-to-all(bf16[32,120,128]{2,1,0:T(8,128)(2,1)S(1)} %fusion.1), channel_id=1, replica_groups={{0,1,2,3,32,33,34,35,64,65,66,67,96,97,98,99,128,129,130,131,160,161,16..., dimensions={0} | all-to-all | bytes 1966080 | tf_op jit(solution)/shard_map/all_to_all | solution.py:290
  46.7 0.1 reduce_sum.12
  46.8 0.8 broadcast_in_dim.6
  47.7 8.2 %all-to-all-start.1 = ((bf16[16,120,128]{2,1,0:T(8,128)(2,1)}), bf16[16,120,128]{2,1,0:T(8,128)(2,1)S(1)}, u32[]{:S(2)}, u32[]{:S(2)}) async-start(bf16[16,120,128]{2,1,0:T(8,128)(2,1)} %broadcast_in_dim.6), calls=%async_computation.1 | async-start | bytes 983040 | tf_op jit(solution)/shard_map/all_to_all | solution.py:292
  55.9 0.0 copy-done.6
  55.9 14.2 %all-to-all-done.1.got_ref = bf16[16,120,128]{2,1,0:T(8,128)(2,1)S(1)} async-done(((bf16[16,120,128]{2,1,0:T(8,128)(2,1)}), bf16[16,120,128]{2,1,0:T(8,128)(2,1)S(1)}, u32[]{:S(2)}, u32[]{:S(2)}) %all-to-all-start.1) | async-done | bytes 491552 | tf_op jit(solution)/shard_map/all_to_all | solution.py:292
  70.1 0.0 copy-done.3
  70.1 12.4 %shampoo.1 = bf16[480,128]{1,0:T(8,128)(2,1)S(1)} custom-call(bf16[16,120,128]{2,1,0:T(8,128)(2,1)S(1)} %all-to-all-done.1.got_ref, f32[180,180]{1,0:T(8,128)S(1)} %bitcast.20, f32[320,320]{1,0:T(8,128)S(1)} %bitcast.21), custom_call_target="tpu_custom_call" | custom-call | tf_op jit(solution)/shard_map/shampoo/pallas_call | solution.py:220
  82.5 0.1 broadcast_in_dim.7
  82.7 17.0 %all_to_all.16.mine_ref = bf16[8,480,128]{2,1,0:T(8,128)(2,1)S(1)} all-to-all(bf16[8,480,128]{2,1,0:T(8,128)(2,1)S(1)} %broadcast_in_dim.7), channel_id=1, replica_groups={{0,32,64,96,128,160,192,224},{16,48,80,112,144,176,208,240},{1,33,65,97..., dimensions={0} | all-to-all | bytes 1966080 | tf_op jit(solution)/shard_map/all_to_all | solution.py:294
  99.6 4.7 %collective-permute-start.1 = (bf16[8,480,128]{2,1,0:T(8,128)(2,1)S(1)}, bf16[8,480,128]{2,1,0:T(8,128)(2,1)S(1)}, u32[]{:S(2)}, u32[]{:S(2)}) collective-permute-start(bf16[8,480,128]{2,1,0:T(8,128)(2,1)S(1)} %all_to_all.16.mine_ref), channel_id=1, source_target_pairs={{0,16},{16,0},{32,48},{48,32},{64,80},{80,64},{96,112},{112,96},{1... | collective-permute-start | bytes 2949128 | tf_op jit(solution)/shard_map/ppermute | solution.py:297
  104.3 2.2 %collective-permute-done.1.theirs_ref = bf16[8,480,128]{2,1,0:T(8,128)(2,1)S(1)} collective-permute-done((bf16[8,480,128]{2,1,0:T(8,128)(2,1)S(1)}, bf16[8,480,128]{2,1,0:T(8,128)(2,1)S(1)}, u32[]{:S(2)}, u32[]{:S(2)}) %collective-permute-start.1) | collective-permute-done | bytes 983072 | tf_op jit(solution)/shard_map/ppermute | solution.py:297
  106.5 2.2 %join.1 = bf16[320,2880]{1,0:T(8,128)(2,1)} custom-call(s32[1]{0:T(128)} %bitcast.core_ref, bf16[8,480,128]{2,1,0:T(8,128)(2,1)S(1)} %all_to_all.16.mine_ref, bf16[8,480,128]{2,1,0:T(8,128)(2,1)S(1)} %collective-permute-done.1.theirs_ref), custom_call_target="tpu_custom_call" | custom-call | tf_op jit(solution)/shard_map/join/pallas_call | solution.py:257
  (1 shorter events, 0.0 us)
Async XLA Ops:
  0.0 1.5 %copy-start = (bf16[2880,320]{0,1:T(8,128)(2,1)S(1)}, bf16[2880,320]{0,1:T(8,128)(2,1)}, u32[]{:S(2)}) copy-start(bf16[2880,320]{0,1:T(8,128)(2,1)} %param.11) | copy-start | bytes 5529604
  1.5 1.4 %copy-start.1 = (bf16[2,32,32,320]{3,2,1,0:T(8,128)(2,1)S(1)}, bf16[2,32,32,320]{3,2,1,0:T(8,128)(2,1)}, u32[]{:S(2)}) copy-start(bf16[2,32,32,320]{3,2,1,0:T(8,128)(2,1)} %param.7) | copy-start | bytes 3932164
  2.9 1.4 %copy-start.2 = (bf16[2,32,32,320]{3,2,1,0:T(8,128)(2,1)S(1)}, bf16[2,32,32,320]{3,2,1,0:T(8,128)(2,1)}, u32[]{:S(2)}) copy-start(bf16[2,32,32,320]{3,2,1,0:T(8,128)(2,1)} %param.8) | copy-start | bytes 3932164
  4.3 0.7 copy-start.4
  5.0 0.7 copy-start.5
  19.2 5.5 %collective-permute-start = (bf16[32,120,128]{2,1,0:T(8,128)(2,1)S(1)}, bf16[32,120,128]{2,1,0:T(8,128)(2,1)S(1)}, u32[]{:S(2)}, u32[]{:S(2)}) collective-permute-start(bf16[32,120,128]{2,1,0:T(8,128)(2,1)S(1)} %fusion.2), channel_id=1, source_target_pairs={{0,16},{16,0},{32,48},{48,32},{64,80},{80,64},{96,112},{112,96},{1... | collective-permute-start | bytes 2949128 | tf_op jit(solution)/shard_map/ppermute | solution.py:288
  24.9 31.0 %copy-start.6 = (f32[1,180,180]{2,0,1:T(1,128)S(1)}, f32[1,180,180]{2,0,1:T(1,128)}, u32[]{:S(2)}) copy-start(f32[1,180,180]{2,0,1:T(1,128)} %param.12) | copy-start | bytes 388804
  24.9 45.2 %copy-start.3 = (f32[1,320,320]{2,1,0:T(8,128)S(1)}, f32[1,320,320]{2,1,0:T(8,128)}, u32[]{:S(2)}) copy-start(f32[1,320,320]{2,1,0:T(8,128)} %param.13) | copy-start | bytes 1228804
  47.7 22.4 %all-to-all-start.1 = ((bf16[16,120,128]{2,1,0:T(8,128)(2,1)}), bf16[16,120,128]{2,1,0:T(8,128)(2,1)S(1)}, u32[]{:S(2)}, u32[]{:S(2)}) async-start(bf16[16,120,128]{2,1,0:T(8,128)(2,1)} %broadcast_in_dim.6), calls=%async_computation.1 | async-start | bytes 983040 | tf_op jit(solution)/shard_map/all_to_all | solution.py:292
  99.6 6.9 %collective-permute-start.1 = (bf16[8,480,128]{2,1,0:T(8,128)(2,1)S(1)}, bf16[8,480,128]{2,1,0:T(8,128)(2,1)S(1)}, u32[]{:S(2)}, u32[]{:S(2)}) collective-permute-start(bf16[8,480,128]{2,1,0:T(8,128)(2,1)S(1)} %all_to_all.16.mine_ref), channel_id=1, source_target_pairs={{0,16},{16,0},{32,48},{48,32},{64,80},{80,64},{96,112},{112,96},{1... | collective-permute-start | bytes 2949128 | tf_op jit(solution)/shard_map/ppermute | solution.py:297

commit v2 on v1

--- a/solution.py
+++ b/solution.py
@@ -25,6 +25,7 @@
 
 VMEM = pl.BlockSpec(memory_space=pltpu.VMEM)
 SMEM = pl.BlockSpec(memory_space=pltpu.SMEM)
+HBM = pl.BlockSpec(memory_space=pltpu.HBM)
 
 
 def dot(a, b, contract=(1, 0)):
@@ -58,50 +59,64 @@
     return jnp.concatenate([packed[:QROWS], right], axis=1)
 
 
-def conv_kernel(total, core_ref, adv_ref, time_ref, lat_ref, tgt_ref, ker_ref, out_ref, wide, kthree, cot, gt, minus):
+def conv_kernel(
+    total, core_ref, adv_hbm, time_hbm, lat_hbm, tgt_hbm, ker_hbm, out_ref,
+    adv, time, lat, tgt, ker, wide, middle, cot, gt, sems,
+):
+    def fetch(source, target, sem):
+        copy = pltpu.make_async_copy(source, target, sems.at[sem])
+        copy.start()
+        return copy
+
+    half = [pl.ds(s * SPOTS, SPOTS) for s in range(2)]
+    get_lat = [fetch(lat_hbm.at[half[0]], lat.at[half[0]], 0)]
+    get_ker = fetch(ker_hbm, ker, 1)
+    get_adv = fetch(adv_hbm, adv, 2)
+    get_time = fetch(time_hbm, time, 3)
+    get_tgt = [fetch(tgt_hbm.at[half[0]], tgt.at[half[0]], 4)]
+    get_lat.append(fetch(lat_hbm.at[half[1]], lat.at[half[1]], 5))
+    get_tgt.append(fetch(tgt_hbm.at[half[1]], tgt.at[half[1]], 6))
+
     zeros = jnp.zeros((SIDE, TRIPLE), bf16)
     for s in range(2):
         wide[s * STRIDE : s * STRIDE + SIDE, :] = zeros
         wide[s * STRIDE + SIDE + SPOTS : (s + 1) * STRIDE, :] = zeros
-    chunk = 128
-    column = lax.broadcasted_iota(jnp.int32, (chunk, C), 0) % SIDE
-
-    for s in range(2):
-
-        def widen(i, carry, s=s):
-            x = lat_ref[pl.ds(pl.multiple_of(s * SPOTS + i * chunk, chunk), chunk), :].astype(f32)
-            before = jnp.where(column == 0, 0.0, pltpu.roll(x, 1, 0))
-            after = jnp.where(column == SIDE - 1, 0.0, pltpu.roll(x, chunk - 1, 0))
-            row = pl.multiple_of(s * STRIDE + SIDE + i * chunk, 32)
-            wide[pl.ds(row, chunk), :] = jnp.concatenate([before, x, after], axis=1).astype(bf16)
-            return carry
-
-        lax.fori_loop(0, SPOTS // chunk, widen, 0)
-    for a in range(3):
-        kthree[a] = ker_ref[:, a * TRIPLE : (a + 1) * TRIPLE]
-    rows = lax.broadcasted_iota(jnp.int32, (C, C), 0)
-    cols = lax.broadcasted_iota(jnp.int32, (C, C), 1)
-    minus[...] = jnp.where(rows == cols, -1.0, 0.0).astype(bf16)
-
     span = 256
-    for s in range(2):
-        weight = jnp.full((1, span), adv_ref[s], f32) / (
-            (0.1 + jnp.full((1, span), time_ref[s], jnp.int32).astype(f32) / STEPS) * total
-        )
-
-        def forward(j, carry, s=s, weight=weight):
-            acc = dot(
-                minus[...],
-                tgt_ref[pl.ds(pl.multiple_of(s * SPOTS + j * span, span), span), :],
-                (1, 1),
-            )
-            for a in range(3):
-                row = pl.multiple_of(s * STRIDE + j * span + a * SIDE, 32)
-                acc = acc + dot(kthree[a], wide[pl.ds(row, span), :], (1, 1))
-            cot[:, pl.ds(pl.multiple_of(s * SPOTS + j * span, span), span)] = (weight * acc).astype(bf16)
-            return carry
-
-        lax.fori_loop(0, SPOTS // span, forward, 0)
+    column = lax.broadcasted_iota(jnp.int32, (span, C), 0) % SIDE
+
+    def widen(j):
+        s, r = divmod(j * span, SPOTS)
+        if r == 0:
+            get_lat[s].wait()
+        x = lat[j * span : (j + 1) * span, :].astype(f32)
+        before = jnp.where(column == 0, 0.0, pltpu.roll(x, 1, 0))
+        after = jnp.where(column == SIDE - 1, 0.0, pltpu.roll(x, span - 1, 0))
+        row = s * STRIDE + SIDE + r
+        wide[row : row + span, :] = jnp.concatenate([before, x, after], axis=1).astype(bf16)
+
+    widen(0)
+    widen(1)
+    get_ker.wait()
+    middle[...] = ker[:, TRIPLE : 2 * TRIPLE]
+    get_adv.wait()
+    get_time.wait()
+    weights = [
+        jnp.full((1, span), adv[s], f32)
+        / ((0.1 + jnp.full((1, span), time[s], jnp.int32).astype(f32) / STEPS) * total)
+        for s in range(2)
+    ]
+    for j in range(2 * SPOTS // span):
+        s, r = divmod(j * span, SPOTS)
+        if r == 0:
+            get_tgt[s].wait()
+        if (j + 2) * span < 2 * SPOTS:
+            widen(j + 2)
+        row = s * STRIDE + r
+        acc = dot(ker[:, :TRIPLE], wide[row : row + span, :], (1, 1))
+        acc = acc + dot(middle[...], wide[row + SIDE : row + SIDE + span, :], (1, 1))
+        acc = acc + dot(ker[:, 2 * TRIPLE :], wide[row + 2 * SIDE : row + 2 * SIDE + span, :], (1, 1))
+        goal = tgt[j * span : (j + 1) * span, :].astype(f32).T
+        cot[:, j * span : (j + 1) * span] = (weights[s] * (acc - goal)).astype(bf16)
 
     for a in range(3):
         for start in range(0, TRIPLE, 256):
@@ -132,16 +147,21 @@
     return pl.pallas_call(
         functools.partial(conv_kernel, total),
         out_shape=jax.ShapeDtypeStruct((2, 32, QPACK, 128), f32),
-        in_specs=[SMEM, SMEM, SMEM, VMEM, VMEM, VMEM],
+        in_specs=[SMEM, HBM, HBM, HBM, HBM, HBM],
         out_specs=VMEM,
         scratch_shapes=[
+            pltpu.SMEM((2,), f32),
+            pltpu.SMEM((2,), jnp.int32),
+            pltpu.VMEM((2 * SPOTS, C), bf16),
+            pltpu.VMEM((2 * SPOTS, C), bf16),
+            pltpu.VMEM((C, ROWS), bf16),
             pltpu.VMEM((2 * STRIDE, TRIPLE), bf16),
-            pltpu.VMEM((3, C, TRIPLE), bf16),
+            pltpu.VMEM((C, TRIPLE), bf16),
             pltpu.VMEM((C, 2 * SPOTS), bf16),
             pltpu.VMEM((3, C, TRIPLE), f32),
-            pltpu.VMEM((C, C), bf16),
+            pltpu.SemaphoreType.DMA((7,)),
         ],
-        compiler_params=pltpu.CompilerParams(vmem_limit_bytes=40 * 1024 * 1024),
+        compiler_params=pltpu.CompilerParams(vmem_limit_bytes=50 * 1024 * 1024),
         name="conv_grad",
     )(core, advantages, timesteps, latents, targets, kernel_t)
 
@@ -177,10 +197,7 @@
 def shampoo_kernel(got_ref, left_ref, right_ref, out_ref, pr, plft, xs):
     quarters = []
     for q in range(4):
-        s = got_ref[q].astype(f32)
-        for z in range(1, 4):
-            s = s + got_ref[4 * z + q].astype(f32)
-        quarters.append(unpack_quarter(s))
+        quarters.append(unpack_quarter(got_ref[q].astype(f32)))
     h = jnp.concatenate(quarters, axis=0)
     ht = h.T
     xs[...] = h
@@ -271,6 +288,8 @@
     for c in range(2)
     for z in range(4)
 ]
+FAR_GROUPS = [[4 * z + q for z in range(4)] for q in range(4)]
+NEAR_GROUPS = [[4 * z + q for q in range(4)] for z in range(4)]
 
 
 def local(latents, targets, advantages, timesteps, kernel, prior_left, prior_right):
@@ -288,8 +307,14 @@
     theirs = lax.ppermute(parts[1].astype(bf16), "own", CORE_SWAP)
     pair = (parts[0] + theirs.astype(f32)).astype(bf16)
     spread = lax.all_to_all(pair, ("own", "rep"), 0, 0, axis_index_groups=WIDE_GROUPS)
-    quarter = jnp.sum(spread.astype(f32), axis=0).astype(bf16)
-    got = lax.all_to_all(jnp.broadcast_to(quarter, (16, QPACK, 128)), "rep", 0, 0)
+    quarter = lax.optimization_barrier(jnp.sum(spread.astype(f32), axis=0)).astype(bf16)
+    far = lax.all_to_all(
+        jnp.broadcast_to(quarter, (4, QPACK, 128)), "rep", 0, 0, axis_index_groups=FAR_GROUPS
+    )
+    quarter = lax.optimization_barrier(jnp.sum(far.astype(f32), axis=0)).astype(bf16)
+    got = lax.all_to_all(
+        jnp.broadcast_to(quarter, (4, QPACK, 128)), "rep", 0, 0, axis_index_groups=NEAR_GROUPS
+    )
     step = shampoo(got, prior_left[0], prior_right[0])
     mine = lax.all_to_all(
         jnp.broadcast_to(step, (8, 4 * QPACK, 128)), "own", 0, 0, axis_index_groups=EIGHTS

time: 109 us -> 109 us (level)
  blocking collectives: 38.7 us -> 51.3 us
  waiting for transfers between devices: 18.6 us -> 7.99 us
  starting transfers between devices: 16.2 us -> 12.6 us
  other arithmetic: 0.37 us -> 1.94 us
    all_to_all x0 -> x1, blocking collectives: none -> 14.3 us  [local(): lax.all_to_all(jnp.broadcast_to(quarter, (4, QPACK, 128)), 'rep', 0, 0, a...]
    all_to_all x1, waiting for transfers between devices: 14.2 us -> 3.6 us  [local(): lax.all_to_all(jnp.broadcast_to(quarter, (4, QPACK, 128)), 'rep', 0, 0, a...]
    all_to_all x1, starting transfers between devices: 8.2 us -> 3.5 us  [local(): lax.all_to_all(jnp.broadcast_to(quarter, (4, QPACK, 128)), 'rep', 0, 0, a...]
    all_to_all x1, blocking collectives: 17 us -> 15.3 us  [local(): lax.all_to_all(jnp.broadcast_to(step, (8, 4 * QPACK, 128)), 'own', 0, 0,...]
    convert_element_type x1, other arithmetic: 0.23 us -> 1.78 us  [local(): pair = (parts[0] + theirs.astype(f32)).astype(bf16)]
    convert_element_type x1, local copies, waits for them, and re-layouts: 0.13 us -> 1.67 us  [local(): theirs = lax.ppermute(parts[1].astype(bf16), 'own', CORE_SWAP)]
    unnamed x15 -> x13, local copies, waits for them, and re-layouts: 5.67 us -> 4.15 us
    ppermute x1, starting transfers between devices: 4.7 us -> 5.82 us  [local(): theirs = lax.ppermute(mine, 'own', CORE_SWAP)]
where the time goes in v2:
time: 109 us; the launch traced here: 108 us
  blocking collectives  51.3 us (47%)
  Pallas kernels  27.8 us (26%)
  starting transfers between devices  12.6 us (12%)
  waiting for transfers between devices  7.99 us (7%)
  local copies, waits for them, and re-layouts  6.64 us (6%)
  other arithmetic  1.94 us (2%)
    all_to_all x1, blocking collectives, local(): lax.all_to_all(pair, ('own', 'rep'), 0, 0, axis_index_groups=WIDE_GROUPS)  21.7 us
    all_to_all x1, blocking collectives, local(): lax.all_to_all(jnp.broadcast_to(step, (8, 4 * QPACK, 128)), 'own', 0, 0,...  15.3 us
    all_to_all x1, blocking collectives, local(): lax.all_to_all(jnp.broadcast_to(quarter, (4, QPACK, 128)), 'rep', 0, 0, a...  14.3 us
    pallas_call x1, Pallas kernels, conv_grad(): pl.pallas_call(functools.partial(conv_kernel, total), out_shape=jax.Shape...  13.2 us
    pallas_call x1, Pallas kernels, shampoo(): pl.pallas_call(shampoo_kernel, out_shape=jax.ShapeDtypeStruct((4 * QPACK,...  12.4 us
    ppermute x1, starting transfers between devices, local(): theirs = lax.ppermute(mine, 'own', CORE_SWAP)  5.82 us
    unnamed x13, local copies, waits for them, and re-layouts  4.15 us
    all_to_all x1, waiting for transfers between devices, local(): lax.all_to_all(jnp.broadcast_to(quarter, (4, QPACK, 128)), 'rep', 0, 0, a...  3.6 us
  transfers between devices with their start and end apart: 3, of which 3 were waited for; matrix products, arithmetic and copies ran while one was open for 0% of the time, Pallas kernels for 0%

profile of v2, /device:TPU:1, one launch (start us, length us, event | category | flops | bytes accessed | tf_op | source)
XLA Modules:
  0.0 108.4 jit_solution(18370205657771328902)
XLA Ops:
  0.0 0.0 copy-start
  0.0 1.4 %copy-done = bf16[2,32,32,320]{3,2,1,0:T(8,128)(2,1)S(1)} copy-done((bf16[2,32,32,320]{3,2,1,0:T(8,128)(2,1)S(1)}, bf16[2,32,32,320]{3,2,1,0:T(8,128)(2,1)}, u32[]{:S(2)}) %copy-start) | copy-done | bytes 1310744
  1.4 0.0 copy-start.1
  1.4 1.4 %copy-done.1 = bf16[2,32,32,320]{3,2,1,0:T(8,128)(2,1)S(1)} copy-done((bf16[2,32,32,320]{3,2,1,0:T(8,128)(2,1)S(1)}, bf16[2,32,32,320]{3,2,1,0:T(8,128)(2,1)}, u32[]{:S(2)}) %copy-start.1) | copy-done | bytes 1310744
  2.8 0.0 copy-start.3
  2.8 0.7 copy-done.3
  3.5 0.0 copy-start.4
  3.5 0.7 copy-done.4
  4.1 13.2 %conv_grad.1 = f32[2,32,120,128]{3,2,1,0:T(8,128)} custom-call(s32[1]{0:T(128)} %bitcast.core_ref, f32[2]{0:T(128)S(1)} %copy-done.3, s32[2]{0:T(128)S(1)} %copy-done.4, bf16[2048,320]{1,0:T(8,128)(2,1)S(1)} %bitcast.17, bf16[2048,320]{1,0:T(8,128)(2,1)S(1)} %bitcast.18, bf16[320,2880]{1,0:T(8,128)(2,1)} %bitcast.21), custom_call_target="tpu_custom_call" | custom-call | tf_op jit(solution)/shard_map/conv_grad/pallas_call | solution.py:147
  17.3 1.7 %fusion.2 = bf16[32,120,128]{2,1,0:T(8,128)(2,1)S(1)} fusion(f32[2,32,120,128]{3,2,1,0:T(8,128)} %conv_grad.1), kind=kLoop, calls=%fused_computation.5 | loop fusion | bytes 1966080 | tf_op jit(solution)/shard_map/convert_element_type | solution.py:307
  19.0 3.3 %collective-permute-start = (bf16[32,120,128]{2,1,0:T(8,128)(2,1)S(1)}, bf16[32,120,128]{2,1,0:T(8,128)(2,1)S(1)}, u32[]{:S(2)}, u32[]{:S(2)}) collective-permute-start(bf16[32,120,128]{2,1,0:T(8,128)(2,1)S(1)} %fusion.2), channel_id=1, source_target_pairs={{0,16},{16,0},{32,48},{48,32},{64,80},{80,64},{96,112},{112,96},{1... | collective-permute-start | bytes 2949128 | tf_op jit(solution)/shard_map/ppermute | solution.py:307
  22.3 2.2 %collective-permute-done = bf16[32,120,128]{2,1,0:T(8,128)(2,1)S(1)} collective-permute-done((bf16[32,120,128]{2,1,0:T(8,128)(2,1)S(1)}, bf16[32,120,128]{2,1,0:T(8,128)(2,1)S(1)}, u32[]{:S(2)}, u32[]{:S(2)}) %collective-permute-start) | collective-permute-done | bytes 983072 | tf_op jit(solution)/shard_map/ppermute | solution.py:307
  24.5 1.8 %fusion.1 = bf16[32,120,128]{2,1,0:T(8,128)(2,1)S(1)} fusion(f32[2,32,120,128]{3,2,1,0:T(8,128)} %conv_grad.1, bf16[32,120,128]{2,1,0:T(8,128)(2,1)S(1)} %collective-permute-done), kind=kLoop, calls=%fused_computation.3 | loop fusion | flops 1474560 | bytes 3932160 | tf_op jit(solution)/shard_map/convert_element_type | solution.py:308
  26.3 0.0 copy-start.5
  26.3 0.0 copy-start.2
  26.3 21.7 %all_to_all.20 = bf16[32,120,128]{2,1,0:T(8,128)(2,1)S(1)} all-to-all(bf16[32,120,128]{2,1,0:T(8,128)(2,1)S(1)} %fusion.1), channel_id=1, replica_groups={{0,1,2,3,32,33,34,35,64,65,66,67,96,97,98,99,128,129,130,131,160,161,16..., dimensions={0} | all-to-all | bytes 1966080 | tf_op jit(solution)/shard_map/all_to_all | solution.py:309
  48.1 0.1 convert_reduce_fusion
  48.2 14.3 %all_to_all.21 = bf16[4,120,128]{2,1,0:T(8,128)(2,1)S(1)} all-to-all(bf16[4,120,128]{2,1,0:T(8,128)(2,1)S(1)} %broadcast_in_dim.9), channel_id=1, replica_groups={{0,4,8,12},{1,5,9,13},{2,6,10,14},{3,7,11,15},{16,20,24,28},{17,21,25,2..., dimensions={0} | all-to-all | bytes 245760 | tf_op jit(solution)/shard_map/all_to_all | solution.py:311
  62.5 0.7 broadcast_in_dim.10
  63.2 3.5 %all-to-all-start.2 = ((bf16[4,120,128]{2,1,0:T(8,128)(2,1)}), bf16[4,120,128]{2,1,0:T(8,128)(2,1)S(1)}, u32[]{:S(2)}, u32[]{:S(2)}) async-start(bf16[4,120,128]{2,1,0:T(8,128)(2,1)} %broadcast_in_dim.10), calls=%async_computation.2 | async-start | bytes 245760 | tf_op jit(solution)/shard_map/all_to_all | solution.py:315
  66.7 0.0 copy-done.5
  66.7 3.6 %all-to-all-done.2.got_ref = bf16[4,120,128]{2,1,0:T(8,128)(2,1)S(1)} async-done(((bf16[4,120,128]{2,1,0:T(8,128)(2,1)}), bf16[4,120,128]{2,1,0:T(8,128)(2,1)S(1)}, u32[]{:S(2)}, u32[]{:S(2)}) %all-to-all-start.2) | async-done | bytes 122912 | tf_op jit(solution)/shard_map/all_to_all | solution.py:315
  70.3 0.0 copy-done.2
  70.3 12.4 %shampoo.1 = bf16[480,128]{1,0:T(8,128)(2,1)S(1)} custom-call(bf16[4,120,128]{2,1,0:T(8,128)(2,1)S(1)} %all-to-all-done.2.got_ref, f32[180,180]{1,0:T(8,128)S(1)} %bitcast.19, f32[320,320]{1,0:T(8,128)S(1)} %bitcast.20), custom_call_target="tpu_custom_call" | custom-call | tf_op jit(solution)/shard_map/shampoo/pallas_call | solution.py:237
  82.7 0.1 broadcast_in_dim.11
  82.8 15.3 %all_to_all.22.mine_ref = bf16[8,480,128]{2,1,0:T(8,128)(2,1)S(1)} all-to-all(bf16[8,480,128]{2,1,0:T(8,128)(2,1)S(1)} %broadcast_in_dim.11), channel_id=1, replica_groups={{0,32,64,96,128,160,192,224},{16,48,80,112,144,176,208,240},{1,33,65,97..., dimensions={0} | all-to-all | bytes 1966080 | tf_op jit(solution)/shard_map/all_to_all | solution.py:319
  98.2 5.8 %collective-permute-start.1 = (bf16[8,480,128]{2,1,0:T(8,128)(2,1)S(1)}, bf16[8,480,128]{2,1,0:T(8,128)(2,1)S(1)}, u32[]{:S(2)}, u32[]{:S(2)}) collective-permute-start(bf16[8,480,128]{2,1,0:T(8,128)(2,1)S(1)} %all_to_all.22.mine_ref), channel_id=1, source_target_pairs={{0,16},{16,0},{32,48},{48,32},{64,80},{80,64},{96,112},{112,96},{1... | collective-permute-start | bytes 2949128 | tf_op jit(solution)/shard_map/ppermute | solution.py:322
  104.0 2.2 %collective-permute-done.1.theirs_ref = bf16[8,480,128]{2,1,0:T(8,128)(2,1)S(1)} collective-permute-done((bf16[8,480,128]{2,1,0:T(8,128)(2,1)S(1)}, bf16[8,480,128]{2,1,0:T(8,128)(2,1)S(1)}, u32[]{:S(2)}, u32[]{:S(2)}) %collective-permute-start.1) | collective-permute-done | bytes 983072 | tf_op jit(solution)/shard_map/ppermute | solution.py:322
  106.2 2.2 %join.1 = bf16[320,2880]{1,0:T(8,128)(2,1)} custom-call(s32[1]{0:T(128)} %bitcast.core_ref, bf16[8,480,128]{2,1,0:T(8,128)(2,1)S(1)} %all_to_all.22.mine_ref, bf16[8,480,128]{2,1,0:T(8,128)(2,1)S(1)} %collective-permute-done.1.theirs_ref), custom_call_target="tpu_custom_call" | custom-call | tf_op jit(solution)/shard_map/join/pallas_call | solution.py:274
  (3 shorter events, 0.1 us)
Async XLA Ops:
  0.0 1.4 %copy-start = (bf16[2,32,32,320]{3,2,1,0:T(8,128)(2,1)S(1)}, bf16[2,32,32,320]{3,2,1,0:T(8,128)(2,1)}, u32[]{:S(2)}) copy-start(bf16[2,32,32,320]{3,2,1,0:T(8,128)(2,1)} %param.7) | copy-start | bytes 3932164
  1.4 1.4 %copy-start.1 = (bf16[2,32,32,320]{3,2,1,0:T(8,128)(2,1)S(1)}, bf16[2,32,32,320]{3,2,1,0:T(8,128)(2,1)}, u32[]{:S(2)}) copy-start(bf16[2,32,32,320]{3,2,1,0:T(8,128)(2,1)} %param.8) | copy-start | bytes 3932164
  2.8 0.7 copy-start.3
  3.5 0.7 copy-start.4
  19.0 5.5 %collective-permute-start = (bf16[32,120,128]{2,1,0:T(8,128)(2,1)S(1)}, bf16[32,120,128]{2,1,0:T(8,128)(2,1)S(1)}, u32[]{:S(2)}, u32[]{:S(2)}) collective-permute-start(bf16[32,120,128]{2,1,0:T(8,128)(2,1)S(1)} %fusion.2), channel_id=1, source_target_pairs={{0,16},{16,0},{32,48},{48,32},{64,80},{80,64},{96,112},{112,96},{1... | collective-permute-start | bytes 2949128 | tf_op jit(solution)/shard_map/ppermute | solution.py:307
  26.3 40.4 %copy-start.5 = (f32[1,180,180]{2,0,1:T(1,128)S(1)}, f32[1,180,180]{2,0,1:T(1,128)}, u32[]{:S(2)}) copy-start(f32[1,180,180]{2,0,1:T(1,128)} %param.12) | copy-start | bytes 388804
  26.3 44.0 %copy-start.2 = (f32[1,320,320]{2,1,0:T(8,128)S(1)}, f32[1,320,320]{2,1,0:T(8,128)}, u32[]{:S(2)}) copy-start(f32[1,320,320]{2,1,0:T(8,128)} %param.13) | copy-start | bytes 1228804
  63.2 7.1 %all-to-all-start.2 = ((bf16[4,120,128]{2,1,0:T(8,128)(2,1)}), bf16[4,120,128]{2,1,0:T(8,128)(2,1)S(1)}, u32[]{:S(2)}, u32[]{:S(2)}) async-start(bf16[4,120,128]{2,1,0:T(8,128)(2,1)} %broadcast_in_dim.10), calls=%async_computation.2 | async-start | bytes 245760 | tf_op jit(solution)/shard_map/all_to_all | solution.py:315
  98.2 8.0 %collective-permute-start.1 = (bf16[8,480,128]{2,1,0:T(8,128)(2,1)S(1)}, bf16[8,480,128]{2,1,0:T(8,128)(2,1)S(1)}, u32[]{:S(2)}, u32[]{:S(2)}) collective-permute-start(bf16[8,480,128]{2,1,0:T(8,128)(2,1)S(1)} %all_to_all.22.mine_ref), channel_id=1, source_target_pairs={{0,16},{16,0},{32,48},{48,32},{64,80},{80,64},{96,112},{112,96},{1... | collective-permute-start | bytes 2949128 | tf_op jit(solution)/shard_map/ppermute | solution.py:322
